TPU v7x, 32 devices: a whole 2x2x4 slice. The times are simulated.
32 devices in a mesh: hier: 8 (over y, x, core), col: 4 (over z).
Axes of the slice: x: 2, y: 2, z: 4, core: 2. Of those that a mesh axis runs over, the one named last changes fastest.
Arguments:
- densities: float32 [32, 2, 256, 256], P('hier', None, 'col'), may hold values from -6 to 6
- hamiltonian: float32 [256, 256], replicated, may hold values from -0.35355339 to 0.35355339, as said below
- couplings: float32 [2, 256, 256], replicated, may hold values from -0.088388348 to 0.088388348, as said below
- gamma: float32 [2], replicated, may hold values from 0.005 to 0.05
- coeff: float32 [2, 2], replicated, may hold values from -0.5 to 0.5
- node_count: int32 [8], replicated, may hold values from 2 to 4, as said below
Outputs:
- new_densities: float32 [32, 2, 256, 256], P('hier', None, 'col')
Inputs may be any that keep to these rules, and one draw needn't show every extreme that they name: `node_count`: at least one index of hier holds 4 nodes; every index holds 2 or more. `hamiltonian`: symmetric. `couplings`: each of the two matrices is symmetric.
All inputs are finite; a program needn't handle non-finite values.
Results may differ from a plain program's by a relative error of at most 0.00012.
Values sent between devices are 32-bit elements; how exact they have to be, the bound alone decides.
A program may use at most 64 MiB of HBM per device.

v0:
```python
import functools

import jax
import jax.numpy as jnp
from jax import lax
from jax.experimental import pallas as pl
from jax.experimental.pallas import tpu as pltpu
from jax.sharding import PartitionSpec as P

DEPTH2 = 2
MESH = pl.DeviceIdType.MESH
step_size = 0.2


def split(value):
    high = value.astype(jnp.bfloat16)
    low = (value - high.astype(jnp.float32)).astype(jnp.bfloat16)
    return high, low


def product(both, high, rhs_high, rhs_low):
    rows = high.shape[0]
    wide = jnp.dot(both, rhs_high, preferred_element_type=jnp.float32)
    rest = jnp.dot(high, rhs_low, preferred_element_type=jnp.float32)
    return wide[:rows] + (wide[rows:] + rest)


def kernel(
    shards,
    ring,
    counts,
    gamma,
    coeff,
    x_hbm,
    h_hbm,
    q_hbm,
    out_ref,
    x_ref,
    h_ref,
    q_ref,
    full,
    mid,
    right_high,
    right_low,
    left_both,
    lefts,
    rights,
    to_upper,
    to_lower,
    from_lower,
    from_upper,
    ring_send,
    ring_recv,
    hop_send,
    hop_recv,
    own_sem,
    load_sem,
):
    slots, _, rows, order = x_hbm.shape
    here = lax.axis_index("hier")
    me = lax.axis_index("col")
    reach = ring // 2
    right = (here, lax.rem(me + 1, ring))
    left = (here, lax.rem(me + ring - 1, ring))
    has_lower = here > 0
    has_upper = here < shards - 1

    loads = [
        pltpu.make_async_copy(source, place, load_sem.at[i])
        for i, (source, place) in enumerate(((x_hbm, x_ref), (h_hbm, h_ref), (q_hbm, q_ref)))
    ]
    for load in loads:
        load.start()

    barrier = pltpu.get_barrier_semaphore()
    for neighbour in (left, right):
        pl.semaphore_signal(barrier, inc=1, device_id=neighbour, device_id_type=MESH)

    @pl.when(has_lower)
    def _():
        pl.semaphore_signal(barrier, inc=1, device_id=(here - 1, me), device_id_type=MESH)

    @pl.when(has_upper)
    def _():
        pl.semaphore_signal(barrier, inc=1, device_id=(here + 1, me), device_id_type=MESH)

    pl.semaphore_wait(barrier, 2 + has_lower.astype(jnp.int32) + has_upper.astype(jnp.int32))

    def panel(origin):
        return pl.ds(pl.multiple_of(lax.rem(origin + ring, ring) * rows, rows), rows)

    def ring_copy(section, way, distance, s, origin):
        first, size = (way, 1) if 2 * distance == ring else (0, 2)
        parts = pl.ds(first, size)
        place = full.at[section, s, parts, panel(origin), :]
        if distance == 1:
            source = (x_hbm if section == 0 else mid).at[s, parts]
        else:
            source = place
        return pltpu.make_async_remote_copy(
            src_ref=source,
            dst_ref=place,
            send_sem=ring_send.at[section, way, distance - 1, s],
            recv_sem=ring_recv.at[section, way, distance - 1, s],
            device_id=right if way == 0 else left,
            device_id_type=MESH,
        )

    def sent(section, way, distance, s):
        origin = me - (distance - 1) if way == 0 else me + (distance - 1)
        return ring_copy(section, way, distance, s, origin)

    def arrived(section, way, distance, s):
        origin = me - distance if way == 0 else me + distance
        return ring_copy(section, way, distance, s, origin)

    def own_copy(section, s):
        source = (x_hbm if section == 0 else mid).at[s]
        return pltpu.make_async_copy(
            source, full.at[section, s, :, panel(me), :], own_sem.at[section, s]
        )

    def hop_copy(section, way):
        source, place = (to_upper, from_lower) if way == 0 else (to_lower, from_upper)
        return pltpu.make_async_remote_copy(
            src_ref=source.at[section],
            dst_ref=place.at[section],
            send_sem=hop_send.at[section, way],
            recv_sem=hop_recv.at[section, way],
            device_id=(here + 1, me) if way == 0 else (here - 1, me),
            device_id_type=MESH,
        )

    def start_slot(section, s):
        for way in range(2):
            sent(section, way, 1, s).start()
        own_copy(section, s).start()

    early, late = range(DEPTH2), range(DEPTH2, slots)
    for s in early:
        start_slot(0, s)

    for section in range(2):

        @pl.when(jnp.logical_not(has_lower))
        def _():
            from_lower[section] = jnp.zeros(from_lower.shape[1:], jnp.float32)

        @pl.when(jnp.logical_not(has_upper))
        def _():
            from_upper[section] = jnp.zeros(from_upper.shape[1:], jnp.float32)

    for load in loads:
        load.wait()
    mine = panel(me)
    for a in range(3):
        high, low = split(h_ref[...] if a == 0 else q_ref[a - 1])
        right_high[a], right_low[a] = high, low
        high, low = split(h_ref[mine, :] if a == 0 else q_ref[a - 1, mine, :])
        left_both[a * rows : (a + 1) * rows] = high
        left_both[(3 + a) * rows : (4 + a) * rows] = low

    offset = jnp.int32(0)
    total = jnp.int32(0)
    count = jnp.int32(0)
    for i in range(shards):
        held = counts[i]
        total = total + held
        offset = offset + jnp.where(here > i, held, 0)
        count = count + jnp.where(here == i, held, 0)
    live_total = total // DEPTH2 * DEPTH2

    def number(flag):
        return jnp.where(flag, jnp.float32(1), jnp.float32(0))

    def root(value):
        return jnp.sqrt(jnp.full((1, order), value, jnp.float32))

    def levels(q):
        node = offset + q
        level = (node + DEPTH2) // DEPTH2 - 1
        return level, node - level * DEPTH2, (node >= 0) & (node < live_total)

    alive, damping = [], []
    for s in range(slots):
        zeroth, first, inside = levels(s)
        alive.append(number(inside & (s < count)))
        damping.append(
            zeroth.astype(jnp.float32) * gamma[0] + first.astype(jnp.float32) * gamma[1]
        )
    edges = range(-DEPTH2, slots + DEPTH2)
    weights = {}
    for q in edges:
        zeroth, first, inside = levels(q)
        target = number(inside)
        base = jnp.maximum(zeroth, 0).astype(jnp.float32)
        above = first.astype(jnp.float32)
        if 0 <= q + DEPTH2 < slots:
            weights[q, "up0"] = root(base + 1.0) * (target * alive[q + DEPTH2])
        if 0 <= q - DEPTH2 < slots:
            weights[q, "down0"] = root(base) * (target * alive[q - DEPTH2])
        if 0 <= q + 1 < slots:
            ok = number(first + 1 < DEPTH2)
            weights[q, "up1"] = root(above + 1.0) * (target * alive[q + 1] * ok)
        if 0 <= q - 1 < slots:
            weights[q, "down1"] = root(above) * (target * alive[q - 1])

    def gathered(q):
        total_re = total_im = None

        def plus(total, term):
            return term if total is None else total + term

        for mode, stride in ((0, DEPTH2), (1, 1)):
            a = mode + 1
            for name, m in (("up", q + stride), ("down", q - stride)):
                if not 0 <= m < slots:
                    continue
                weight = weights[q, f"{name}{mode}"]
                left_re = lefts[m, 0, a * rows : (a + 1) * rows]
                left_im = lefts[m, 1, a * rows : (a + 1) * rows]
                right_re, right_im = rights[m, 0, a], rights[m, 1, a]
                if name == "up":
                    total_re = plus(total_re, weight * (left_re - right_re))
                    total_im = plus(total_im, weight * (left_im - right_im))
                else:
                    real = weight * coeff[mode, 0]
                    imag = weight * coeff[mode, 1]
                    total_re = plus(
                        total_re, real * (left_re - right_re) - imag * (left_im + right_im)
                    )
                    total_im = plus(
                        total_im, real * (left_im - right_im) + imag * (left_re + right_re)
                    )
        return total_re, total_im

    left_high = left_both[: 3 * rows]

    def right_products(section, chosen):
        state = x_ref if section == 0 else mid
        first, size = chosen[0], len(chosen)
        value = state[first : first + size].reshape(size * 2 * rows, order)
        high, low = split(value)
        both = jnp.concatenate([high, low], axis=0)
        for a in range(3):
            value = product(both, high, right_high[a], right_low[a])
            rights[first : first + size, :, a] = value.reshape(size, 2, rows, order)

    def forward(section, s):
        for distance in range(1, reach):
            for way in range(2):
                arrived(section, way, distance, s).wait_recv()
            for way in range(2):
                sent(section, way, distance + 1, s).start()

    def finish(section, s):
        own_copy(section, s).wait()
        for way in range(2):
            arrived(section, way, reach, s).wait_recv()
        for p in range(2):
            high, low = split(full[section, s, p])
            lefts[s, p] = product(left_both[...], left_high, high, low)

    def send_lower(section):
        for q in range(-DEPTH2, 0):
            value = gathered(q)
            for p in range(2):
                to_lower[section, q + DEPTH2, p] = value[p]

        @pl.when(has_lower)
        def _():
            hop_copy(section, 1).start()

    def send_upper(section, near):
        for j in range(DEPTH2):
            for p in range(2):
                value = None
                for q in range(DEPTH2 + j, slots + j + 1):
                    term = number(count + j == q) * near[q][p]
                    value = term if value is None else value + term
                to_upper[section, j, p] = value

        @pl.when(has_upper)
        def _():
            hop_copy(section, 0).start()

    def wait_upper(section):
        @pl.when(has_upper)
        def _():
            hop_copy(section, 1).wait_recv()

    def wait_lower(section):
        @pl.when(has_lower)
        def _():
            hop_copy(section, 0).wait_recv()

    def update(section, s, near):
        state = x_ref if section == 0 else mid
        parts = []
        for p in range(2):
            value = lefts[s, p, :rows] - rights[s, p, 0] + near[s][p]
            if s < DEPTH2:
                value = value + from_lower[section, s, p]
            for j in range(DEPTH2):
                value = value + number(s == count - DEPTH2 + j) * from_upper[section, j, p]
            parts.append(value)
        slope_re = (parts[1] - damping[s] * state[s, 0]) * alive[s]
        slope_im = (-parts[0] - damping[s] * state[s, 1]) * alive[s]
        place, length = (mid, 0.5 * step_size) if section == 0 else (out_ref, step_size)
        place[s, 0] = x_ref[s, 0] + length * slope_re
        place[s, 1] = x_ref[s, 1] + length * slope_im

    right_products(0, range(slots))
    for i, s in enumerate(early):
        forward(0, s)
        if DEPTH2 + i < slots:
            start_slot(0, DEPTH2 + i)
    for s in range(slots):
        if s >= 1 and s + DEPTH2 - 1 < slots:
            forward(0, s + DEPTH2 - 1)
        if s == DEPTH2:
            send_lower(0)
        finish(0, s)
    near = {q: gathered(q) for q in range(DEPTH2, slots + DEPTH2)}
    send_upper(0, near)
    wait_upper(0)
    for s in late:
        update(0, s, near)
        start_slot(1, s)
    near = {q: gathered(q) for q in early}
    for s in late:
        forward(1, s)
    wait_lower(0)
    for s in early:
        update(0, s, near)
        start_slot(1, s)
    right_products(1, early)
    right_products(1, late)
    for s in late:
        finish(1, s)
    for s in early:
        forward(1, s)
    for s in early:
        finish(1, s)
    send_lower(1)
    near = {q: gathered(q) for q in range(DEPTH2, slots + DEPTH2)}
    send_upper(1, near)
    near.update({q: gathered(q) for q in early})
    wait_upper(1)
    wait_lower(1)
    for s in range(slots):
        update(1, s, near)

    for section in range(2):
        for s in range(slots):
            for distance in range(1, reach + 1):
                for way in range(2):
                    sent(section, way, distance, s).wait_send()

        @pl.when(has_lower)
        def _():
            hop_copy(section, 1).wait_send()

        @pl.when(has_upper)
        def _():
            hop_copy(section, 0).wait_send()


def solution(mesh):
    shards, ring = mesh.shape["hier"], mesh.shape["col"]

    def on_device(densities, hamiltonian, couplings, gamma, coeff, node_count):
        slots, _, rows, order = densities.shape
        f32, bf16 = jnp.float32, jnp.bfloat16
        vmem = pl.BlockSpec(memory_space=pltpu.VMEM)
        smem = pl.BlockSpec(memory_space=pltpu.SMEM)
        edge = (2, DEPTH2, 2, rows, order)
        dma = pltpu.SemaphoreType.DMA
        return pl.pallas_call(
            functools.partial(kernel, shards, ring),
            out_shape=jax.ShapeDtypeStruct(densities.shape, f32),
            in_specs=[smem] * 3 + [pl.BlockSpec(memory_space=pltpu.HBM)] * 3,
            out_specs=vmem,
            scratch_shapes=[
                pltpu.VMEM((slots, 2, rows, order), f32),
                pltpu.VMEM((order, order), f32),
                pltpu.VMEM((2, order, order), f32),
                pltpu.VMEM((2, slots, 2, order, order), f32),
                pltpu.VMEM((slots, 2, rows, order), f32),
                pltpu.VMEM((3, order, order), bf16),
                pltpu.VMEM((3, order, order), bf16),
                pltpu.VMEM((6 * rows, order), bf16),
                pltpu.VMEM((slots, 2, 3 * rows, order), f32),
                pltpu.VMEM((slots, 2, 3, rows, order), f32),
                pltpu.VMEM(edge, f32),
                pltpu.VMEM(edge, f32),
                pltpu.VMEM(edge, f32),
                pltpu.VMEM(edge, f32),
                dma((2, 2, ring // 2, slots)),
                dma((2, 2, ring // 2, slots)),
                dma((2, 2)),
                dma((2, 2)),
                dma((2, slots)),
                dma((3,)),
            ],
            compiler_params=pltpu.CompilerParams(
                collective_id=0, has_side_effects=True, vmem_limit_bytes=67_043_328
            ),
        )(node_count, gamma, coeff, densities, hamiltonian, couplings)

    return jax.shard_map(
        on_device,
        mesh=mesh,
        in_specs=(P("hier", None, "col", None), P(), P(), P(), P(), P()),
        out_specs=P("hier", None, "col", None),
        check_vma=False,
    )
```

profile of v0, /device:TPU:1, one launch (start us, length us, event | category | flops | bytes accessed | tf_op | source)
XLA Modules:
  0.0 90.2 jit_solution(12689368498538816452)
XLA Ops:
  0.0 88.3 %shard_map.64 = f32[4,2,64,256]{3,2,1,0:T(8,128)} custom-call(s32[8]{0:T(128)} %counts.1, f32[2]{0:T(128)} %gamma.1, f32[2,2]{1,0:T(2,128)} %coeff.1, f32[4,2,64,256]{3,2,1,0:T(8,128)} %x_hbm.1, f32[256,256]{1,0:T(8,128)} %h_hbm.1, f32[2,256,256]{2,1,0:T(8,128)} %q_hbm.1), custom_call_target="tpu_custom_call" | custom-call | tf_op jit(solution)/shard_map/pallas_call | solution.py:379
  88.3 1.9 %copy.8 = f32[4,2,64,256]{3,2,1,0:T(8,128)} copy(f32[4,2,64,256]{3,2,1,0:T(8,128)} %shard_map.64) | data formatting | bytes 1048576
where the time goes:
time: 90.4 us; the launch traced here: 90.2 us
  Pallas kernels  88.3 us (98%)
  local copies, waits for them, and re-layouts  1.87 us (2%)
    pallas_call x1, Pallas kernels, on_device(): pl.pallas_call(functools.partial(kernel, shards, ring), out_shape=jax.Sha...  88.3 us
    unnamed x1, local copies, waits for them, and re-layouts  1.87 us

commit v1 on v0

v1 whole, which is shorter than its diff:
```python
import functools

import jax
import jax.numpy as jnp
from jax import lax
from jax.experimental import pallas as pl
from jax.experimental.pallas import tpu as pltpu
from jax.sharding import PartitionSpec as P

DEPTH2 = 2
REACH = 2 * DEPTH2
MESH = pl.DeviceIdType.MESH
step_size = 0.2
second = step_size * 0.5 * step_size


def split(value):
    high = value.astype(jnp.bfloat16)
    low = (value - high.astype(jnp.float32)).astype(jnp.bfloat16)
    return high, low


def product(high, low, rhs_high, rhs_low):
    rows = high.shape[0]
    both = jnp.concatenate([high, low], axis=0)
    wide = jnp.dot(both, rhs_high, preferred_element_type=jnp.float32)
    rest = jnp.dot(high, rhs_low, preferred_element_type=jnp.float32)
    return wide[:rows] + (wide[rows:] + rest)


def number(flag):
    return jnp.where(flag, jnp.float32(1), jnp.float32(0))


def kernel(
    shards,
    ring,
    counts,
    gamma,
    coeff,
    x_hbm,
    h_hbm,
    q_hbm,
    out_ref,
    x_ref,
    h_ref,
    q_ref,
    near_out,
    far_out,
    near_in,
    far_in,
    nodes,
    raised,
    right_high,
    right_low,
    mixed_high,
    mixed_low,
    turned,
    drive,
    decay,
    coupled,
    left_high,
    left_low,
    stack_high,
    stack_low,
    sums,
    own,
    from_left,
    from_right,
    hop_send,
    hop_recv,
    line_send,
    line_recv,
    load_sem,
):
    slots, _, rows, order = x_hbm.shape
    here = lax.axis_index("hier")
    me = lax.axis_index("col")
    has_lower = here > 0
    has_upper = here < shards - 1
    has_left = me > 0
    has_right = me < ring - 1
    f32 = jnp.float32

    loads = [
        pltpu.make_async_copy(source, place, load_sem.at[i])
        for i, (source, place) in enumerate(((x_hbm, x_ref), (h_hbm, h_ref), (q_hbm, q_ref)))
    ]
    for load in loads:
        load.start()

    barrier = pltpu.get_barrier_semaphore()
    neighbours = (
        (has_left, (here, me - 1)),
        (has_right, (here, me + 1)),
        (has_lower, (here - 1, me)),
        (has_upper, (here + 1, me)),
    )
    greeted = jnp.int32(0)
    for exists, device in neighbours:

        @pl.when(exists)
        def _():
            pl.semaphore_signal(barrier, inc=1, device_id=device, device_id_type=MESH)

        greeted = greeted + exists.astype(jnp.int32)
    pl.semaphore_wait(barrier, greeted)

    def hop_copy(stage, way):
        if stage == 0:
            source = near_out if way == 0 else x_hbm.at[pl.ds(0, DEPTH2)]
            place = near_in.at[way]
        else:
            source, place = far_out.at[way], far_in.at[way]
        return pltpu.make_async_remote_copy(
            src_ref=source,
            dst_ref=place,
            send_sem=hop_send.at[stage, way],
            recv_sem=hop_recv.at[stage, way],
            device_id=(here + 1, me) if way == 0 else (here - 1, me),
            device_id_type=MESH,
        )

    def hop_exists(way):
        return has_upper if way == 0 else has_lower

    def hop_comes(way):
        return has_lower if way == 0 else has_upper

    @pl.when(has_lower)
    def _():
        hop_copy(0, 1).start()

    for way in range(2):

        @pl.when(jnp.logical_not(hop_comes(way)))
        def _():
            near_in[way] = jnp.zeros(near_in.shape[1:], f32)
            far_in[way] = jnp.zeros(far_in.shape[1:], f32)

    offset = jnp.int32(0)
    total = jnp.int32(0)
    count = jnp.int32(0)
    for i in range(shards):
        held = counts[i]
        total = total + held
        offset = offset + jnp.where(here > i, held, 0)
        count = count + jnp.where(here == i, held, 0)
    live_total = total // DEPTH2 * DEPTH2
    tops = live_total // DEPTH2
    is_count = {c: number(count == c) for c in range(slots // 2, slots + 1)}

    def levels(k):
        node = offset + k
        level = (node + REACH) // DEPTH2 - REACH // DEPTH2
        return level, node - level * DEPTH2, number((node >= 0) & (node < live_total))

    def root(value):
        return jnp.sqrt(jnp.full((1, order), value, f32))

    zeroth, first, inside, damping = {}, {}, {}, {}
    for k in range(-REACH, slots + REACH):
        zeroth[k], first[k], inside[k] = levels(k)
        damping[k] = zeroth[k].astype(f32) * gamma[0] + first[k].astype(f32) * gamma[1]
    weights = {}
    for k in range(-DEPTH2, slots + DEPTH2):
        base = jnp.maximum(zeroth[k], 0).astype(f32)
        above = first[k].astype(f32)
        ok = number(first[k] + 1 < DEPTH2)
        weights[k, 0] = (
            root(base + 1.0) * (inside[k] * inside[k + DEPTH2]),
            root(base) * (inside[k] * inside[k - DEPTH2]),
        )
        weights[k, 1] = (
            root(above + 1.0) * (inside[k] * inside[k + 1] * ok),
            root(above) * (inside[k] * inside[k - 1]),
        )

    def mixes(array, shift, k, mode):
        stride = DEPTH2 if mode == 0 else 1
        rise, fall = weights[k, mode]
        up, down = k + stride + shift, k - stride + shift
        up_re, up_im = array[up, 0], array[up, 1]
        down_re, down_im = array[down, 0], array[down, 1]
        real, imag = fall * coeff[mode, 0], fall * coeff[mode, 1]
        base_re = rise * up_re + real * down_re
        base_im = rise * up_im + real * down_im
        turn_re, turn_im = imag * down_im, imag * down_re
        plain = (base_re - turn_re, base_im + turn_im)
        conjugate = (base_re + turn_re, base_im - turn_im)
        return plain, conjugate

    def put_mixed(k, a, value):
        for p in range(2):
            high, low = split(value[p])
            at = pl.ds(p * rows, rows), pl.ds(a * order, order)
            mixed_high[(k + DEPTH2,) + at] = high
            mixed_low[(k + DEPTH2,) + at] = low

    def right_product(k, size):
        at = k + DEPTH2
        value = product(
            mixed_high[at : at + size].reshape(size * 2 * rows, 3 * order),
            mixed_low[at : at + size].reshape(size * 2 * rows, 3 * order),
            right_high[...],
            right_low[...],
        )
        return value.reshape(size, 2, rows, order)

    loads[0].wait()
    for j in range(DEPTH2):
        for p in range(2):
            value = None
            for c in is_count:
                term = is_count[c] * x_ref[c - 1 - j, p]
                value = term if value is None else value + term
            near_out[j, p] = value

    @pl.when(has_upper)
    def _():
        hop_copy(0, 0).start()

    for load in loads[1:]:
        load.wait()

    mine = pl.ds(pl.multiple_of(me * rows, rows), rows)
    for a in range(3):
        high, low = split(h_ref[...] if a == 0 else q_ref[a - 1])
        right_high[a * order : (a + 1) * order] = high
        right_low[a * order : (a + 1) * order] = low
    factors = [h_ref[mine, :], q_ref[0, mine, :], q_ref[1, mine, :]]
    high, low = split(jnp.concatenate(factors, axis=0))
    twice = []
    for a in range(3):
        at = slice(a * order, (a + 1) * order)
        value = product(high, low, right_high[at], right_low[at])
        twice.append([value[b * rows : (b + 1) * rows] for b in range(3)])
    blocks = factors + [
        -second * twice[0][0],
        -second * (twice[0][1] + twice[1][0]),
        -second * (twice[0][2] + twice[2][0]),
        -second * (twice[1][2] + twice[2][1]),
        -second * twice[1][1],
        -second * twice[2][2],
    ]
    high, low = split(jnp.concatenate(blocks, axis=0).T)
    left_high[...] = high
    left_low[...] = low

    high, low = split(x_ref[...].reshape(slots * 2 * rows, order))
    for mode in range(2):
        at = slice((mode + 1) * order, (mode + 2) * order)
        value = product(high, low, right_high[at], right_low[at])
        coupled[mode] = value.reshape(slots, 2, rows, order)

    @pl.when(has_lower)
    def _():
        hop_copy(0, 0).wait_recv()

    for j in range(DEPTH2):
        for p in range(2):
            nodes[REACH - 1 - j, p] = near_in[0, j, p] * inside[-1 - j]
            nodes[REACH + j, p] = x_ref[j, p] * inside[j]
    for j in range(DEPTH2):
        for p in range(2):
            value = None
            for c in is_count:
                term = is_count[c] * nodes[REACH + c - 1 - DEPTH2 - j, p]
                value = term if value is None else value + term
            far_out[0, j, p] = value

    @pl.when(has_upper)
    def _():
        hop_copy(1, 0).start()
        hop_copy(0, 1).wait_recv()

    def upper_near(k, p):
        value = None
        for c in is_count:
            if 0 <= k - c < DEPTH2:
                term = is_count[c] * near_in[1, k - c, p]
                value = term if value is None else value + term
        return value

    def upper_far(k, p):
        value = None
        for c in is_count:
            if DEPTH2 <= k - c < REACH:
                term = is_count[c] * far_in[1, k - c - DEPTH2, p]
                value = term if value is None else value + term
        return value

    for k in range(DEPTH2, slots):
        for p in range(2):
            value = x_ref[k, p] * number(k < count) + upper_near(k, p)
            nodes[REACH + k, p] = value * inside[k]
            far_out[1, k - DEPTH2, p] = value

    @pl.when(has_lower)
    def _():
        hop_copy(1, 1).start()
        hop_copy(1, 0).wait_recv()

    @pl.when(has_upper)
    def _():
        hop_copy(1, 1).wait_recv()

    for j in range(DEPTH2):
        for p in range(2):
            nodes[REACH - 1 - DEPTH2 - j, p] = far_in[0, j, p] * inside[-1 - DEPTH2 - j]
    for k in range(slots, slots + REACH):
        for p in range(2):
            near, far = upper_near(k, p), upper_far(k, p)
            value = far if near is None else near if far is None else near + far
            nodes[REACH + k, p] = value * inside[k]

    wide = range(-DEPTH2, slots + DEPTH2)

    def put_stack(s, a, value):
        for p in range(2):
            high, low = split(value[p])
            at = pl.ds(a * rows, rows), pl.ds(p * order, order)
            stack_high[(s,) + at] = high
            stack_low[(s,) + at] = low

    for k in wide:
        plain, conjugate = mixes(nodes, REACH, k, 0)
        for p in range(2):
            raised[k + DEPTH2, p] = plain[p]
        put_mixed(k, 0, (nodes[k + REACH, 0], nodes[k + REACH, 1]))
        put_mixed(k, 1, conjugate)
        plain, conjugate = mixes(nodes, REACH, k, 1)
        put_mixed(k, 2, conjugate)
        if 0 <= k < slots:
            put_stack(k, 5, plain)
    turned[...] = right_product(-DEPTH2, slots + 2 * DEPTH2)

    for k in wide:
        at = k + DEPTH2
        beta = second * damping[k] - step_size
        x_re, x_im = nodes[k + REACH, 0], nodes[k + REACH, 1]
        drive[at, 0] = (2 * second) * turned[at, 0] - beta * x_im
        drive[at, 1] = (2 * second) * turned[at, 1] + beta * x_re
        decay[at, 0] = (second * damping[k]) * x_im - second * turned[at, 0]
        decay[at, 1] = -(second * damping[k]) * x_re - second * turned[at, 1]

    def line_copy(way, q, s):
        place = from_left if way == 0 else from_right
        return pltpu.make_async_remote_copy(
            src_ref=sums.at[s, pl.ds(q * rows, rows), :],
            dst_ref=place.at[q, s],
            send_sem=line_send.at[way, q, s],
            recv_sem=line_recv.at[way, q, s],
            device_id=(here, me + 1) if way == 0 else (here, me - 1),
            device_id_type=MESH,
        )

    for s in range(slots):
        at = s + DEPTH2
        tilt = second * damping[s]
        x_re, x_im = nodes[s + REACH, 0], nodes[s + REACH, 1]
        put_stack(s, 0, (drive[at, 0] - tilt * x_im, drive[at, 1] + tilt * x_re))
        top = zeroth[s].astype(f32)
        edge = (
            number(zeroth[s] + 1 < tops) * (top + 1.0) - top,
            number(first[s] + 1 < DEPTH2) * (first[s].astype(f32) + 1.0) - first[s].astype(f32),
        )
        for mode in range(2):
            plain, _ = mixes(drive, DEPTH2, s, mode)
            if mode == 0:
                linked = raised[at, 0], raised[at, 1]
            else:
                linked, _ = mixes(nodes, REACH, s, 1)
            turn = 2 * second * coeff[mode, 1] * edge[mode]
            put_stack(
                s,
                mode + 1,
                (
                    plain[0] - tilt * linked[1] - turn * coupled[mode, s, 1],
                    plain[1] + tilt * linked[0] + turn * coupled[mode, s, 0],
                ),
            )
        put_stack(s, 3, (x_re, x_im))
        put_stack(s, 4, (raised[at, 0], raised[at, 1]))
        plain, _ = mixes(raised, DEPTH2, s, 1)
        put_stack(s, 6, plain)
        plain, _ = mixes(raised, DEPTH2, s, 0)
        put_stack(s, 7, plain)
        real, imag = coeff[1, 0], coeff[1, 1]
        put_stack(s, 8, (real * x_re - imag * x_im, real * x_im + imag * x_re))
        high = stack_high[s]
        sums[s] = product(left_high[...], left_low[...], high, stack_low[s])

        @pl.when(jnp.logical_not(has_left))
        def _():
            line_copy(0, ring - 1, s).start()

        @pl.when(jnp.logical_not(has_right))
        def _():
            line_copy(1, 0, s).start()

    for i in range(1, ring - 1):
        for s in range(slots):

            @pl.when(jnp.logical_not(has_left))
            def _():
                line_copy(0, ring - 1 - i, s).start()

            @pl.when(jnp.logical_not(has_right))
            def _():
                line_copy(1, i, s).start()

    for s in range(slots):
        put_mixed(s, 0, (decay[s + DEPTH2, 0], decay[s + DEPTH2, 1]))
        for mode in range(2):
            _, conjugate = mixes(decay, DEPTH2, s, mode)
            put_mixed(s, mode + 1, conjugate)
    own[...] = right_product(0, slots)
    for s in range(slots):
        at = s + DEPTH2
        rate = damping[s]
        keep = 1.0 - step_size * rate + second * rate * rate
        beta = step_size - second * rate
        alive = inside[s] * number(s < count)
        own_re = own[s, 0] + keep * nodes[s + REACH, 0] - beta * turned[at, 1]
        own_im = own[s, 1] + keep * nodes[s + REACH, 1] + beta * turned[at, 0]
        out_ref[s, 0] = alive * (own_re + sums[s, mine, :order]) + (1.0 - alive) * x_ref[s, 0]
        out_ref[s, 1] = alive * (own_im + sums[s, mine, order:]) + (1.0 - alive) * x_ref[s, 1]

    def pass_on(way, q, s):
        place = from_left if way == 0 else from_right
        comes = has_left if way == 0 else has_right
        before = me < q if way == 0 else me > q
        line = pl.ds(q * rows, rows)

        @pl.when(comes & before)
        def _():
            line_copy(way, q, s).wait_recv()
            sums[s, line, :] = sums[s, line, :] + place[q, s]
            line_copy(way, q, s).start()

        @pl.when(comes & (me == q))
        def _():
            line_copy(way, q, s).wait_recv()
            alive = inside[s] * number(s < count)
            out_ref[s, 0] = out_ref[s, 0] + alive * place[q, s, :, :order]
            out_ref[s, 1] = out_ref[s, 1] + alive * place[q, s, :, order:]

    for i in range(ring - 1):
        for s in range(slots):
            pass_on(0, ring - 1 - i, s)
            pass_on(1, i, s)

    for stage in range(2):
        for way in range(2):

            @pl.when(hop_exists(way))
            def _():
                hop_copy(stage, way).wait_send()

    for i in range(ring - 1):
        for s in range(slots):

            @pl.when(me < ring - 1 - i)
            def _():
                line_copy(0, ring - 1 - i, s).wait_send()

            @pl.when(me > i)
            def _():
                line_copy(1, i, s).wait_send()


def solution(mesh):
    shards, ring = mesh.shape["hier"], mesh.shape["col"]

    def on_device(densities, hamiltonian, couplings, gamma, coeff, node_count):
        slots, _, rows, order = densities.shape
        f32, bf16 = jnp.float32, jnp.bfloat16
        vmem = pl.BlockSpec(memory_space=pltpu.VMEM)
        smem = pl.BlockSpec(memory_space=pltpu.SMEM)
        dma = pltpu.SemaphoreType.DMA
        wide = slots + 2 * DEPTH2
        block = (2, rows, order)
        return pl.pallas_call(
            functools.partial(kernel, shards, ring),
            out_shape=jax.ShapeDtypeStruct(densities.shape, f32),
            in_specs=[smem] * 3 + [pl.BlockSpec(memory_space=pltpu.HBM)] * 3,
            out_specs=vmem,
            scratch_shapes=[
                pltpu.VMEM((slots, *block), f32),
                pltpu.VMEM((order, order), f32),
                pltpu.VMEM((2, order, order), f32),
                pltpu.VMEM((DEPTH2, *block), f32),
                pltpu.VMEM((2, DEPTH2, *block), f32),
                pltpu.VMEM((2, DEPTH2, *block), f32),
                pltpu.VMEM((2, DEPTH2, *block), f32),
                pltpu.VMEM((slots + 2 * REACH, *block), f32),
                pltpu.VMEM((wide, *block), f32),
                pltpu.VMEM((3 * order, order), bf16),
                pltpu.VMEM((3 * order, order), bf16),
                pltpu.VMEM((wide, 2 * rows, 3 * order), bf16),
                pltpu.VMEM((wide, 2 * rows, 3 * order), bf16),
                pltpu.VMEM((wide, *block), f32),
                pltpu.VMEM((wide, *block), f32),
                pltpu.VMEM((wide, *block), f32),
                pltpu.VMEM((2, slots, *block), f32),
                pltpu.VMEM((order, 9 * rows), bf16),
                pltpu.VMEM((order, 9 * rows), bf16),
                pltpu.VMEM((slots, 9 * rows, 2 * order), bf16),
                pltpu.VMEM((slots, 9 * rows, 2 * order), bf16),
                pltpu.VMEM((slots, order, 2 * order), f32),
                pltpu.VMEM((slots, *block), f32),
                pltpu.VMEM((ring, slots, rows, 2 * order), f32),
                pltpu.VMEM((ring, slots, rows, 2 * order), f32),
                dma((2, 2)),
                dma((2, 2)),
                dma((2, ring, slots)),
                dma((2, ring, slots)),
                dma((3,)),
            ],
            compiler_params=pltpu.CompilerParams(
                collective_id=0, has_side_effects=True, vmem_limit_bytes=67_043_328
            ),
        )(node_count, gamma, coeff, densities, hamiltonian, couplings)

    return jax.shard_map(
        on_device,
        mesh=mesh,
        in_specs=(P("hier", None, "col", None), P(), P(), P(), P(), P()),
        out_specs=P("hier", None, "col", None),
        check_vma=False,
    )
```

time: 90.4 us -> 94 us (1.040)
  the two profiles are of different devices: /device:TPU:1 before, /device:TPU:12 now
where the time goes in v1:
time: 94 us; the launch traced here: 93.8 us
  Pallas kernels  91.9 us (98%)
  local copies, waits for them, and re-layouts  1.87 us (2%)
    pallas_call x1, Pallas kernels, on_device(): pl.pallas_call(functools.partial(kernel, shards, ring), out_shape=jax.Sha...  91.9 us

profile of v1, /device:TPU:12, one launch (start us, length us, event | category | flops | bytes accessed | tf_op | source)
XLA Modules:
  0.0 93.8 jit_solution(7581849929916265052)
XLA Ops:
  0.0 91.9 %shard_map.64 = f32[4,2,64,256]{3,2,1,0:T(8,128)} custom-call(s32[8]{0:T(128)} %counts.1, f32[2]{0:T(128)} %gamma.1, f32[2,2]{1,0:T(2,128)} %coeff.1, f32[4,2,64,256]{3,2,1,0:T(8,128)} %x_hbm.1, f32[256,256]{1,0:T(8,128)} %h_hbm.1, f32[2,256,256]{2,1,0:T(8,128)} %q_hbm.1), custom_call_target="tpu_custom_call" | custom-call | tf_op jit(solution)/shard_map/pallas_call | solution.py:484
  91.9 1.9 %copy.8 = f32[4,2,64,256]{3,2,1,0:T(8,128)} copy(f32[4,2,64,256]{3,2,1,0:T(8,128)} %shard_map.64) | data formatting | bytes 1048576

commit v2 on v1

--- a/solution.py
+++ b/solution.py
@@ -9,6 +9,8 @@
 
 DEPTH2 = 2
 REACH = 2 * DEPTH2
+WINDOW = 3
+LAG = 2
 MESH = pl.DeviceIdType.MESH
 step_size = 0.2
 second = step_size * 0.5 * step_size
@@ -235,7 +237,7 @@
         at = slice(a * order, (a + 1) * order)
         value = product(high, low, right_high[at], right_low[at])
         twice.append([value[b * rows : (b + 1) * rows] for b in range(3)])
-    blocks = factors + [
+    parts = factors + [
         -second * twice[0][0],
         -second * (twice[0][1] + twice[1][0]),
         -second * (twice[0][2] + twice[2][0]),
@@ -243,7 +245,7 @@
         -second * twice[1][1],
         -second * twice[2][2],
     ]
-    high, low = split(jnp.concatenate(blocks, axis=0).T)
+    high, low = split(jnp.concatenate(parts, axis=0).T)
     left_high[...] = high
     left_low[...] = low
 
@@ -344,16 +346,41 @@
         decay[at, 0] = (second * damping[k]) * x_im - second * turned[at, 0]
         decay[at, 1] = -(second * damping[k]) * x_re - second * turned[at, 1]
 
+    def panel(q):
+        return pl.ds(pl.multiple_of(q * rows, rows), rows)
+
     def line_copy(way, q, s):
         place = from_left if way == 0 else from_right
         return pltpu.make_async_remote_copy(
-            src_ref=sums.at[s, pl.ds(q * rows, rows), :],
+            src_ref=sums.at[s, panel(q), :],
             dst_ref=place.at[q, s],
             send_sem=line_send.at[way, q, s],
             recv_sem=line_recv.at[way, q, s],
             device_id=(here, me + 1) if way == 0 else (here, me - 1),
             device_id_type=MESH,
         )
+
+    blocks = (ring - 1) * slots
+
+    def end_copy(way, j):
+        q = j // slots
+        return line_copy(way, ring - 1 - q if way == 0 else q, lax.rem(j, slots))
+
+    def feed_one(way, j):
+        @pl.when((j >= WINDOW) & (j < blocks + WINDOW))
+        def _():
+            end_copy(way, j - WINDOW).wait_send()
+
+        @pl.when(j < blocks)
+        def _():
+            end_copy(way, j).start()
+
+    def feed(j):
+        for way, inner in ((0, has_left), (1, has_right)):
+
+            @pl.when(jnp.logical_not(inner))
+            def _():
+                feed_one(way, jnp.int32(j))
 
     for s in range(slots):
         at = s + DEPTH2
@@ -391,24 +418,7 @@
         high = stack_high[s]
         sums[s] = product(left_high[...], left_low[...], high, stack_low[s])
 
-        @pl.when(jnp.logical_not(has_left))
-        def _():
-            line_copy(0, ring - 1, s).start()
-
-        @pl.when(jnp.logical_not(has_right))
-        def _():
-            line_copy(1, 0, s).start()
-
-    for i in range(1, ring - 1):
-        for s in range(slots):
-
-            @pl.when(jnp.logical_not(has_left))
-            def _():
-                line_copy(0, ring - 1 - i, s).start()
-
-            @pl.when(jnp.logical_not(has_right))
-            def _():
-                line_copy(1, i, s).start()
+        feed(s)
 
     for s in range(slots):
         put_mixed(s, 0, (decay[s + DEPTH2, 0], decay[s + DEPTH2, 1]))
@@ -427,29 +437,41 @@
         out_ref[s, 0] = alive * (own_re + sums[s, mine, :order]) + (1.0 - alive) * x_ref[s, 0]
         out_ref[s, 1] = alive * (own_im + sums[s, mine, order:]) + (1.0 - alive) * x_ref[s, 1]
 
-    def pass_on(way, q, s):
+    def pass_on(way, t):
         place = from_left if way == 0 else from_right
-        comes = has_left if way == 0 else has_right
-        before = me < q if way == 0 else me > q
-        line = pl.ds(q * rows, rows)
-
-        @pl.when(comes & before)
+        passed = me if way == 0 else ring - 1 - me
+        j = t - LAG * passed
+        inner = (passed > 0) & (j >= 0)
+        s = lax.rem(jnp.maximum(j, 0), slots)
+        step = jnp.maximum(j, 0) // slots
+        q = ring - 1 - step if way == 0 else step
+
+        @pl.when(inner & (step < ring - 1 - passed))
         def _():
+            line = panel(q)
             line_copy(way, q, s).wait_recv()
             sums[s, line, :] = sums[s, line, :] + place[q, s]
             line_copy(way, q, s).start()
 
-        @pl.when(comes & (me == q))
+        @pl.when(inner & (step == ring - 1 - passed))
         def _():
             line_copy(way, q, s).wait_recv()
-            alive = inside[s] * number(s < count)
+            alive = number((offset + s < live_total) & (s < count))
             out_ref[s, 0] = out_ref[s, 0] + alive * place[q, s, :, :order]
             out_ref[s, 1] = out_ref[s, 1] + alive * place[q, s, :, order:]
 
-    for i in range(ring - 1):
-        for s in range(slots):
-            pass_on(0, ring - 1 - i, s)
-            pass_on(1, i, s)
+    def advance(t, carry):
+        for way, passed in ((0, me), (1, ring - 1 - me)):
+
+            @pl.when((passed == 0) & (t >= slots))
+            def _():
+                feed_one(way, t)
+
+        for way in range(2):
+            pass_on(way, t)
+        return carry
+
+    lax.fori_loop(0, blocks + max(WINDOW, LAG * (ring - 1)), advance, 0)
 
     for stage in range(2):
         for way in range(2):
@@ -461,11 +483,11 @@
     for i in range(ring - 1):
         for s in range(slots):
 
-            @pl.when(me < ring - 1 - i)
+            @pl.when(has_left & (me < ring - 1 - i))
             def _():
                 line_copy(0, ring - 1 - i, s).wait_send()
 
-            @pl.when(me > i)
+            @pl.when(has_right & (me > i))
             def _():
                 line_copy(1, i, s).wait_send()
 

time: 94 us -> 59.2 us (0.63)
  the two profiles are of different devices: /device:TPU:12 before, /device:TPU:20 now
where the time goes in v2:
time: 59.2 us; the launch traced here: 59 us
  Pallas kernels  57.2 us (97%)
  local copies, waits for them, and re-layouts  1.87 us (3%)
    pallas_call x1, Pallas kernels, on_device(): pl.pallas_call(functools.partial(kernel, shards, ring), out_shape=jax.Sha...  57.2 us
    unnamed x1, local copies, waits for them, and re-layouts  1.87 us

profile of v2, /device:TPU:20, one launch (start us, length us, event | category | flops | bytes accessed | tf_op | source)
XLA Modules:
  0.0 59.0 jit_solution(14956987776377290641)
XLA Ops:
  0.0 57.2 %shard_map.64 = f32[4,2,64,256]{3,2,1,0:T(8,128)} custom-call(s32[8]{0:T(128)} %counts.1, f32[2]{0:T(128)} %gamma.1, f32[2,2]{1,0:T(2,128)} %coeff.1, f32[4,2,64,256]{3,2,1,0:T(8,128)} %x_hbm.1, f32[256,256]{1,0:T(8,128)} %h_hbm.1, f32[2,256,256]{2,1,0:T(8,128)} %q_hbm.1), custom_call_target="tpu_custom_call" | custom-call | tf_op jit(solution)/shard_map/pallas_call | solution.py:506
  57.2 1.9 %copy.8 = f32[4,2,64,256]{3,2,1,0:T(8,128)} copy(f32[4,2,64,256]{3,2,1,0:T(8,128)} %shard_map.64) | data formatting | bytes 1048576

commit v3 on v2

--- a/solution.py
+++ b/solution.py
@@ -11,6 +11,8 @@
 REACH = 2 * DEPTH2
 WINDOW = 3
 LAG = 2
+NEAR_AT = 3
+FAR_AT = 6
 MESH = pl.DeviceIdType.MESH
 step_size = 0.2
 second = step_size * 0.5 * step_size
@@ -63,12 +65,15 @@
     coupled,
     left_high,
     left_low,
+    raw_in,
     stack_high,
     stack_low,
     sums,
     own,
     from_left,
     from_right,
+    raw_send,
+    raw_recv,
     hop_send,
     hop_recv,
     line_send,
@@ -108,17 +113,31 @@
         greeted = greeted + exists.astype(jnp.int32)
     pl.semaphore_wait(barrier, greeted)
 
-    def hop_copy(stage, way):
+    edge = (me == 1) | (me == ring - 2)
+    end = jnp.where(me == 1, 0, ring - 1)
+
+    def raw_copy(s):
+        return pltpu.make_async_remote_copy(
+            src_ref=x_hbm.at[s],
+            dst_ref=raw_in.at[s],
+            send_sem=raw_send.at[s],
+            recv_sem=raw_recv.at[s],
+            device_id=(here, jnp.where(me == 0, 1, ring - 2)),
+            device_id_type=MESH,
+        )
+
+    def hop_copy(turn, stage, way):
         if stage == 0:
-            source = near_out if way == 0 else x_hbm.at[pl.ds(0, DEPTH2)]
-            place = near_in.at[way]
+            first = (x_hbm if turn == 0 else raw_in).at[pl.ds(0, DEPTH2)]
+            source = near_out.at[turn] if way == 0 else first
+            place = near_in.at[turn, way]
         else:
-            source, place = far_out.at[way], far_in.at[way]
+            source, place = far_out.at[turn, way], far_in.at[turn, way]
         return pltpu.make_async_remote_copy(
             src_ref=source,
             dst_ref=place,
-            send_sem=hop_send.at[stage, way],
-            recv_sem=hop_recv.at[stage, way],
+            send_sem=hop_send.at[turn, stage, way],
+            recv_sem=hop_recv.at[turn, stage, way],
             device_id=(here + 1, me) if way == 0 else (here - 1, me),
             device_id_type=MESH,
         )
@@ -131,14 +150,20 @@
 
     @pl.when(has_lower)
     def _():
-        hop_copy(0, 1).start()
-
-    for way in range(2):
-
-        @pl.when(jnp.logical_not(hop_comes(way)))
-        def _():
-            near_in[way] = jnp.zeros(near_in.shape[1:], f32)
-            far_in[way] = jnp.zeros(far_in.shape[1:], f32)
+        hop_copy(0, 0, 1).start()
+
+    @pl.when(jnp.logical_not(has_left & has_right))
+    def _():
+        for s in range(slots):
+            raw_copy(s).start()
+
+    for turn in range(2):
+        for way in range(2):
+
+            @pl.when(jnp.logical_not(hop_comes(way)))
+            def _():
+                near_in[turn, way] = jnp.zeros(near_in.shape[2:], f32)
+                far_in[turn, way] = jnp.zeros(far_in.shape[2:], f32)
 
     offset = jnp.int32(0)
     total = jnp.int32(0)
@@ -209,18 +234,21 @@
         )
         return value.reshape(size, 2, rows, order)
 
+    def send_near(turn, state):
+        for j in range(DEPTH2):
+            for p in range(2):
+                value = None
+                for c in is_count:
+                    term = is_count[c] * state[c - 1 - j, p]
+                    value = term if value is None else value + term
+                near_out[turn, j, p] = value
+
+        @pl.when(has_upper)
+        def _():
+            hop_copy(turn, 0, 0).start()
+
     loads[0].wait()
-    for j in range(DEPTH2):
-        for p in range(2):
-            value = None
-            for c in is_count:
-                term = is_count[c] * x_ref[c - 1 - j, p]
-                value = term if value is None else value + term
-            near_out[j, p] = value
-
-    @pl.when(has_upper)
-    def _():
-        hop_copy(0, 0).start()
+    send_near(0, x_ref)
 
     for load in loads[1:]:
         load.wait()
@@ -230,91 +258,108 @@
         high, low = split(h_ref[...] if a == 0 else q_ref[a - 1])
         right_high[a * order : (a + 1) * order] = high
         right_low[a * order : (a + 1) * order] = low
-    factors = [h_ref[mine, :], q_ref[0, mine, :], q_ref[1, mine, :]]
-    high, low = split(jnp.concatenate(factors, axis=0))
-    twice = []
-    for a in range(3):
-        at = slice(a * order, (a + 1) * order)
-        value = product(high, low, right_high[at], right_low[at])
-        twice.append([value[b * rows : (b + 1) * rows] for b in range(3)])
-    parts = factors + [
-        -second * twice[0][0],
-        -second * (twice[0][1] + twice[1][0]),
-        -second * (twice[0][2] + twice[2][0]),
-        -second * (twice[1][2] + twice[2][1]),
-        -second * twice[1][1],
-        -second * twice[2][2],
-    ]
-    high, low = split(jnp.concatenate(parts, axis=0).T)
-    left_high[...] = high
-    left_low[...] = low
-
-    high, low = split(x_ref[...].reshape(slots * 2 * rows, order))
-    for mode in range(2):
-        at = slice((mode + 1) * order, (mode + 2) * order)
-        value = product(high, low, right_high[at], right_low[at])
-        coupled[mode] = value.reshape(slots, 2, rows, order)
-
-    @pl.when(has_lower)
+
+    def left_factors(turn, lines):
+        factors = [h_ref[lines, :], q_ref[0, lines, :], q_ref[1, lines, :]]
+        high, low = split(jnp.concatenate(factors, axis=0))
+        twice = []
+        for a in range(3):
+            at = slice(a * order, (a + 1) * order)
+            value = product(high, low, right_high[at], right_low[at])
+            twice.append([value[b * rows : (b + 1) * rows] for b in range(3)])
+        parts = factors + [
+            -second * twice[0][0],
+            -second * (twice[0][1] + twice[1][0]),
+            -second * (twice[0][2] + twice[2][0]),
+            -second * (twice[1][2] + twice[2][1]),
+            -second * twice[1][1],
+            -second * twice[2][2],
+        ]
+        high, low = split(jnp.concatenate(parts, axis=0).T)
+        left_high[turn] = high
+        left_low[turn] = low
+
+    left_factors(0, mine)
+
+    @pl.when(edge)
     def _():
-        hop_copy(0, 0).wait_recv()
-
-    for j in range(DEPTH2):
-        for p in range(2):
-            nodes[REACH - 1 - j, p] = near_in[0, j, p] * inside[-1 - j]
-            nodes[REACH + j, p] = x_ref[j, p] * inside[j]
-    for j in range(DEPTH2):
-        for p in range(2):
-            value = None
-            for c in is_count:
-                term = is_count[c] * nodes[REACH + c - 1 - DEPTH2 - j, p]
-                value = term if value is None else value + term
-            far_out[0, j, p] = value
-
-    @pl.when(has_upper)
-    def _():
-        hop_copy(1, 0).start()
-        hop_copy(0, 1).wait_recv()
-
-    def upper_near(k, p):
+        left_factors(1, pl.ds(pl.multiple_of(end * rows, rows), rows))
+
+    def couple(state):
+        high, low = split(state[...].reshape(slots * 2 * rows, order))
+        for mode in range(2):
+            at = slice((mode + 1) * order, (mode + 2) * order)
+            value = product(high, low, right_high[at], right_low[at])
+            coupled[mode] = value.reshape(slots, 2, rows, order)
+
+    couple(x_ref)
+
+    def upper_near(turn, k, p):
         value = None
         for c in is_count:
             if 0 <= k - c < DEPTH2:
-                term = is_count[c] * near_in[1, k - c, p]
+                term = is_count[c] * near_in[turn, 1, k - c, p]
                 value = term if value is None else value + term
         return value
 
-    def upper_far(k, p):
+    def upper_far(turn, k, p):
         value = None
         for c in is_count:
             if DEPTH2 <= k - c < REACH:
-                term = is_count[c] * far_in[1, k - c - DEPTH2, p]
+                term = is_count[c] * far_in[turn, 1, k - c - DEPTH2, p]
                 value = term if value is None else value + term
         return value
 
-    for k in range(DEPTH2, slots):
-        for p in range(2):
-            value = x_ref[k, p] * number(k < count) + upper_near(k, p)
-            nodes[REACH + k, p] = value * inside[k]
-            far_out[1, k - DEPTH2, p] = value
-
-    @pl.when(has_lower)
-    def _():
-        hop_copy(1, 1).start()
-        hop_copy(1, 0).wait_recv()
-
-    @pl.when(has_upper)
-    def _():
-        hop_copy(1, 1).wait_recv()
-
-    for j in range(DEPTH2):
-        for p in range(2):
-            nodes[REACH - 1 - DEPTH2 - j, p] = far_in[0, j, p] * inside[-1 - DEPTH2 - j]
-    for k in range(slots, slots + REACH):
-        for p in range(2):
-            near, far = upper_near(k, p), upper_far(k, p)
-            value = far if near is None else near if far is None else near + far
-            nodes[REACH + k, p] = value * inside[k]
+    def gather_near(turn, state):
+        @pl.when(has_lower)
+        def _():
+            hop_copy(turn, 0, 0).wait_recv()
+
+        for j in range(DEPTH2):
+            for p in range(2):
+                nodes[REACH - 1 - j, p] = near_in[turn, 0, j, p] * inside[-1 - j]
+                nodes[REACH + j, p] = state[j, p] * inside[j]
+        for j in range(DEPTH2):
+            for p in range(2):
+                value = None
+                for c in is_count:
+                    term = is_count[c] * nodes[REACH + c - 1 - DEPTH2 - j, p]
+                    value = term if value is None else value + term
+                far_out[turn, 0, j, p] = value
+
+        @pl.when(has_upper)
+        def _():
+            hop_copy(turn, 1, 0).start()
+            hop_copy(turn, 0, 1).wait_recv()
+
+        for k in range(DEPTH2, slots):
+            for p in range(2):
+                value = state[k, p] * number(k < count) + upper_near(turn, k, p)
+                nodes[REACH + k, p] = value * inside[k]
+                far_out[turn, 1, k - DEPTH2, p] = value
+
+        @pl.when(has_lower)
+        def _():
+            hop_copy(turn, 1, 1).start()
+
+    def gather_far(turn):
+        @pl.when(has_lower)
+        def _():
+            hop_copy(turn, 1, 0).wait_recv()
+
+        @pl.when(has_upper)
+        def _():
+            hop_copy(turn, 1, 1).wait_recv()
+
+        for j in range(DEPTH2):
+            for p in range(2):
+                at = REACH - 1 - DEPTH2 - j
+                nodes[at, p] = far_in[turn, 0, j, p] * inside[-1 - DEPTH2 - j]
+        for k in range(slots, slots + REACH):
+            for p in range(2):
+                near, far = upper_near(turn, k, p), upper_far(turn, k, p)
+                value = far if near is None else near if far is None else near + far
+                nodes[REACH + k, p] = value * inside[k]
 
     wide = range(-DEPTH2, slots + DEPTH2)
 
@@ -325,26 +370,42 @@
             stack_high[(s,) + at] = high
             stack_low[(s,) + at] = low
 
-    for k in wide:
-        plain, conjugate = mixes(nodes, REACH, k, 0)
-        for p in range(2):
-            raised[k + DEPTH2, p] = plain[p]
-        put_mixed(k, 0, (nodes[k + REACH, 0], nodes[k + REACH, 1]))
-        put_mixed(k, 1, conjugate)
-        plain, conjugate = mixes(nodes, REACH, k, 1)
-        put_mixed(k, 2, conjugate)
-        if 0 <= k < slots:
-            put_stack(k, 5, plain)
-    turned[...] = right_product(-DEPTH2, slots + 2 * DEPTH2)
-
-    for k in wide:
-        at = k + DEPTH2
-        beta = second * damping[k] - step_size
-        x_re, x_im = nodes[k + REACH, 0], nodes[k + REACH, 1]
-        drive[at, 0] = (2 * second) * turned[at, 0] - beta * x_im
-        drive[at, 1] = (2 * second) * turned[at, 1] + beta * x_re
-        decay[at, 0] = (second * damping[k]) * x_im - second * turned[at, 0]
-        decay[at, 1] = -(second * damping[k]) * x_re - second * turned[at, 1]
+    def mix_nodes():
+        for k in wide:
+            plain, conjugate = mixes(nodes, REACH, k, 0)
+            for p in range(2):
+                raised[k + DEPTH2, p] = plain[p]
+            put_mixed(k, 0, (nodes[k + REACH, 0], nodes[k + REACH, 1]))
+            put_mixed(k, 1, conjugate)
+            plain, conjugate = mixes(nodes, REACH, k, 1)
+            put_mixed(k, 2, conjugate)
+            if 0 <= k < slots:
+                put_stack(k, 5, plain)
+
+    def turn_nodes(first, size):
+        turned[first + DEPTH2 : first + DEPTH2 + size] = right_product(first, size)
+        for k in range(first, first + size):
+            at = k + DEPTH2
+            beta = second * damping[k] - step_size
+            x_re, x_im = nodes[k + REACH, 0], nodes[k + REACH, 1]
+            drive[at, 0] = (2 * second) * turned[at, 0] - beta * x_im
+            drive[at, 1] = (2 * second) * turned[at, 1] + beta * x_re
+
+    gather_near(0, x_ref)
+    gather_far(0)
+    mix_nodes()
+    turn_nodes(-DEPTH2, slots + 2 * DEPTH2)
+
+    @pl.when(edge)
+    def _():
+        for s in range(slots):
+            raw_copy(s).wait_recv()
+
+        @pl.when(has_lower)
+        def _():
+            hop_copy(1, 0, 1).start()
+
+        send_near(1, raw_in)
 
     def panel(q):
         return pl.ds(pl.multiple_of(q * rows, rows), rows)
@@ -360,7 +421,7 @@
             device_id_type=MESH,
         )
 
-    blocks = (ring - 1) * slots
+    blocks = (ring - 2) * slots
 
     def end_copy(way, j):
         q = j // slots
@@ -382,13 +443,13 @@
             def _():
                 feed_one(way, jnp.int32(j))
 
-    for s in range(slots):
+    def fill_stack(s):
         at = s + DEPTH2
         tilt = second * damping[s]
         x_re, x_im = nodes[s + REACH, 0], nodes[s + REACH, 1]
         put_stack(s, 0, (drive[at, 0] - tilt * x_im, drive[at, 1] + tilt * x_re))
         top = zeroth[s].astype(f32)
-        edge = (
+        lift = (
             number(zeroth[s] + 1 < tops) * (top + 1.0) - top,
             number(first[s] + 1 < DEPTH2) * (first[s].astype(f32) + 1.0) - first[s].astype(f32),
         )
@@ -398,7 +459,7 @@
                 linked = raised[at, 0], raised[at, 1]
             else:
                 linked, _ = mixes(nodes, REACH, s, 1)
-            turn = 2 * second * coeff[mode, 1] * edge[mode]
+            turn = 2 * second * coeff[mode, 1] * lift[mode]
             put_stack(
                 s,
                 mode + 1,
@@ -415,11 +476,17 @@
         put_stack(s, 7, plain)
         real, imag = coeff[1, 0], coeff[1, 1]
         put_stack(s, 8, (real * x_re - imag * x_im, real * x_im + imag * x_re))
-        high = stack_high[s]
-        sums[s] = product(left_high[...], left_low[...], high, stack_low[s])
-
+
+    for s in range(slots):
+        fill_stack(s)
+        sums[s] = product(left_high[0], left_low[0], stack_high[s], stack_low[s])
         feed(s)
 
+    for k in wide:
+        at = k + DEPTH2
+        x_re, x_im = nodes[k + REACH, 0], nodes[k + REACH, 1]
+        decay[at, 0] = (second * damping[k]) * x_im - second * turned[at, 0]
+        decay[at, 1] = -(second * damping[k]) * x_re - second * turned[at, 1]
     for s in range(slots):
         put_mixed(s, 0, (decay[s + DEPTH2, 0], decay[s + DEPTH2, 1]))
         for mode in range(2):
@@ -441,7 +508,7 @@
         place = from_left if way == 0 else from_right
         passed = me if way == 0 else ring - 1 - me
         j = t - LAG * passed
-        inner = (passed > 0) & (j >= 0)
+        inner = (passed > 0) & (j >= 0) & (j < blocks)
         s = lax.rem(jnp.maximum(j, 0), slots)
         step = jnp.maximum(j, 0) // slots
         q = ring - 1 - step if way == 0 else step
@@ -471,14 +538,56 @@
             pass_on(way, t)
         return carry
 
-    lax.fori_loop(0, blocks + max(WINDOW, LAG * (ring - 1)), advance, 0)
+    def act(s):
+        fill_stack(s)
+        value = product(left_high[1, mine, :], left_low[1, mine, :], stack_high[s], stack_low[s])
+        alive = inside[s] * number(s < count)
+        out_ref[s, 0] = out_ref[s, 0] + alive * value[:, :order]
+        out_ref[s, 1] = out_ref[s, 1] + alive * value[:, order:]
+
+    def extra_near():
+        gather_near(1, raw_in)
+        couple(raw_in)
+
+    def extra_far():
+        gather_far(1)
+        mix_nodes()
+
+    half = slots // 2 + DEPTH2
+    extras = (
+        (NEAR_AT, extra_near),
+        (FAR_AT, extra_far),
+        (FAR_AT + 1, functools.partial(turn_nodes, -DEPTH2, half)),
+        (FAR_AT + 2, functools.partial(turn_nodes, half - DEPTH2, half)),
+        (FAR_AT + 3, lambda: [act(s) for s in range(slots // 2)]),
+        (FAR_AT + 4, lambda: [act(s) for s in range(slots // 2, slots)]),
+    )
+    begin = 0
+    for at, extra in extras:
+        lax.fori_loop(begin, at, advance, 0)
+        begin = at
+
+        @pl.when(edge)
+        def _():
+            extra()
+
+    lax.fori_loop(begin, blocks + max(WINDOW, LAG * (ring - 1)), advance, 0)
+
+    @pl.when(jnp.logical_not(has_left & has_right))
+    def _():
+        for s in range(slots):
+            raw_copy(s).wait_send()
 
     for stage in range(2):
         for way in range(2):
 
             @pl.when(hop_exists(way))
             def _():
-                hop_copy(stage, way).wait_send()
+                hop_copy(0, stage, way).wait_send()
+
+            @pl.when(hop_exists(way) & edge)
+            def _():
+                hop_copy(1, stage, way).wait_send()
 
     for i in range(ring - 1):
         for s in range(slots):
@@ -512,10 +621,10 @@
                 pltpu.VMEM((slots, *block), f32),
                 pltpu.VMEM((order, order), f32),
                 pltpu.VMEM((2, order, order), f32),
-                pltpu.VMEM((DEPTH2, *block), f32),
                 pltpu.VMEM((2, DEPTH2, *block), f32),
-                pltpu.VMEM((2, DEPTH2, *block), f32),
-                pltpu.VMEM((2, DEPTH2, *block), f32),
+                pltpu.VMEM((2, 2, DEPTH2, *block), f32),
+                pltpu.VMEM((2, 2, DEPTH2, *block), f32),
+                pltpu.VMEM((2, 2, DEPTH2, *block), f32),
                 pltpu.VMEM((slots + 2 * REACH, *block), f32),
                 pltpu.VMEM((wide, *block), f32),
                 pltpu.VMEM((3 * order, order), bf16),
@@ -526,16 +635,19 @@
                 pltpu.VMEM((wide, *block), f32),
                 pltpu.VMEM((wide, *block), f32),
                 pltpu.VMEM((2, slots, *block), f32),
-                pltpu.VMEM((order, 9 * rows), bf16),
-                pltpu.VMEM((order, 9 * rows), bf16),
+                pltpu.VMEM((2, order, 9 * rows), bf16),
+                pltpu.VMEM((2, order, 9 * rows), bf16),
+                pltpu.VMEM((slots, *block), f32),
                 pltpu.VMEM((slots, 9 * rows, 2 * order), bf16),
                 pltpu.VMEM((slots, 9 * rows, 2 * order), bf16),
                 pltpu.VMEM((slots, order, 2 * order), f32),
                 pltpu.VMEM((slots, *block), f32),
                 pltpu.VMEM((ring, slots, rows, 2 * order), f32),
                 pltpu.VMEM((ring, slots, rows, 2 * order), f32),
-                dma((2, 2)),
-                dma((2, 2)),
+                dma((slots,)),
+                dma((slots,)),
+                dma((2, 2, 2)),
+                dma((2, 2, 2)),
                 dma((2, ring, slots)),
                 dma((2, ring, slots)),
                 dma((3,)),

time: 59.2 us -> 53.2 us (0.90)
  the two profiles are of different devices: /device:TPU:20 before, /device:TPU:12 now
where the time goes in v3:
time: 53.2 us; the launch traced here: 53 us
  Pallas kernels  51.1 us (96%)
  local copies, waits for them, and re-layouts  1.87 us (4%)
    pallas_call x1, Pallas kernels, on_device(): pl.pallas_call(functools.partial(kernel, shards, ring), out_shape=jax.Sha...  51.1 us
    unnamed x1, local copies, waits for them, and re-layouts  1.87 us

profile of v3, /device:TPU:12, one launch (start us, length us, event | category | flops | bytes accessed | tf_op | source)
XLA Modules:
  0.0 53.0 jit_solution(7402633267171953314)
XLA Ops:
  0.0 51.1 %shard_map.64 = f32[4,2,64,256]{3,2,1,0:T(8,128)} custom-call(s32[8]{0:T(128)} %counts.1, f32[2]{0:T(128)} %gamma.1, f32[2,2]{1,0:T(2,128)} %coeff.1, f32[4,2,64,256]{3,2,1,0:T(8,128)} %x_hbm.1, f32[256,256]{1,0:T(8,128)} %h_hbm.1, f32[2,256,256]{2,1,0:T(8,128)} %q_hbm.1), custom_call_target="tpu_custom_call" | custom-call | tf_op jit(solution)/shard_map/pallas_call | solution.py:615
  51.1 1.9 %copy.8 = f32[4,2,64,256]{3,2,1,0:T(8,128)} copy(f32[4,2,64,256]{3,2,1,0:T(8,128)} %shard_map.64) | data formatting | bytes 1048576

commit v4 on v3

--- a/solution.py
+++ b/solution.py
@@ -9,10 +9,11 @@
 
 DEPTH2 = 2
 REACH = 2 * DEPTH2
-WINDOW = 3
+WINDOW = 4
 LAG = 2
-NEAR_AT = 3
-FAR_AT = 6
+OWN_AT = 3
+NEAR_AT = 5
+FAR_AT = 8
 MESH = pl.DeviceIdType.MESH
 step_size = 0.2
 second = step_size * 0.5 * step_size
@@ -70,6 +71,7 @@
     stack_low,
     sums,
     own,
+    total,
     from_left,
     from_right,
     raw_send,
@@ -166,20 +168,23 @@
                 far_in[turn, way] = jnp.zeros(far_in.shape[2:], f32)
 
     offset = jnp.int32(0)
-    total = jnp.int32(0)
+    nodes_held = jnp.int32(0)
     count = jnp.int32(0)
     for i in range(shards):
         held = counts[i]
-        total = total + held
+        nodes_held = nodes_held + held
         offset = offset + jnp.where(here > i, held, 0)
         count = count + jnp.where(here == i, held, 0)
-    live_total = total // DEPTH2 * DEPTH2
+    live_total = nodes_held // DEPTH2 * DEPTH2
     tops = live_total // DEPTH2
     is_count = {c: number(count == c) for c in range(slots // 2, slots + 1)}
 
+    start = offset + count - slots
+    margin = REACH + slots
+
     def levels(k):
-        node = offset + k
-        level = (node + REACH) // DEPTH2 - REACH // DEPTH2
+        node = start + k
+        level = (node + margin) // DEPTH2 - margin // DEPTH2
         return level, node - level * DEPTH2, number((node >= 0) & (node < live_total))
 
     def root(value):
@@ -285,81 +290,85 @@
     def _():
         left_factors(1, pl.ds(pl.multiple_of(end * rows, rows), rows))
 
-    def couple(state):
-        high, low = split(state[...].reshape(slots * 2 * rows, order))
+    def couple():
+        here_nodes = nodes[REACH : REACH + slots]
+        high, low = split(here_nodes.reshape(slots * 2 * rows, order))
         for mode in range(2):
             at = slice((mode + 1) * order, (mode + 2) * order)
             value = product(high, low, right_high[at], right_low[at])
             coupled[mode] = value.reshape(slots, 2, rows, order)
 
-    couple(x_ref)
-
-    def upper_near(turn, k, p):
+    def chosen(term_of):
         value = None
         for c in is_count:
-            if 0 <= k - c < DEPTH2:
-                term = is_count[c] * near_in[turn, 1, k - c, p]
+            term = term_of(c)
+            if term is not None:
+                term = is_count[c] * term
                 value = term if value is None else value + term
         return value
 
-    def upper_far(turn, k, p):
-        value = None
-        for c in is_count:
-            if DEPTH2 <= k - c < REACH:
-                term = is_count[c] * far_in[turn, 1, k - c - DEPTH2, p]
-                value = term if value is None else value + term
-        return value
+    def below(turn, d, p):
+        if d > REACH:
+            return None
+        if d > DEPTH2:
+            return far_in[turn, 0, d - 1 - DEPTH2, p]
+        return near_in[turn, 0, d - 1, p]
 
     def gather_near(turn, state):
         @pl.when(has_lower)
         def _():
             hop_copy(turn, 0, 0).wait_recv()
 
+        for k in range(slots):
+            for p in range(2):
+
+                def held(c):
+                    at = k + c - slots
+                    return state[at, p] if at >= 0 else below(turn, -at, p)
+
+                nodes[REACH + k, p] = chosen(held) * inside[k]
         for j in range(DEPTH2):
             for p in range(2):
-                nodes[REACH - 1 - j, p] = near_in[turn, 0, j, p] * inside[-1 - j]
-                nodes[REACH + j, p] = state[j, p] * inside[j]
+                far_out[turn, 0, j, p] = nodes[REACH + slots - 1 - DEPTH2 - j, p]
+
+        @pl.when(has_upper)
+        def _():
+            hop_copy(turn, 1, 0).start()
+            hop_copy(turn, 0, 1).wait_recv()
+
         for j in range(DEPTH2):
             for p in range(2):
-                value = None
-                for c in is_count:
-                    term = is_count[c] * nodes[REACH + c - 1 - DEPTH2 - j, p]
-                    value = term if value is None else value + term
-                far_out[turn, 0, j, p] = value
-
-        @pl.when(has_upper)
-        def _():
-            hop_copy(turn, 1, 0).start()
-            hop_copy(turn, 0, 1).wait_recv()
-
-        for k in range(DEPTH2, slots):
+                nodes[REACH + slots + j, p] = near_in[turn, 1, j, p] * inside[slots + j]
+                at = DEPTH2 + j
+
+                def next_node(c):
+                    return state[at, p] if at < c else near_in[turn, 1, at - c, p]
+
+                far_out[turn, 1, j, p] = chosen(next_node)
+
+        @pl.when(has_lower)
+        def _():
+            hop_copy(turn, 1, 1).start()
+
+    def gather_below(turn):
+        @pl.when(has_lower)
+        def _():
+            hop_copy(turn, 1, 0).wait_recv()
+
+        for d in range(1, REACH + 1):
             for p in range(2):
-                value = state[k, p] * number(k < count) + upper_near(turn, k, p)
-                nodes[REACH + k, p] = value * inside[k]
-                far_out[turn, 1, k - DEPTH2, p] = value
-
-        @pl.when(has_lower)
-        def _():
-            hop_copy(turn, 1, 1).start()
-
-    def gather_far(turn):
-        @pl.when(has_lower)
-        def _():
-            hop_copy(turn, 1, 0).wait_recv()
-
+                value = chosen(lambda c: below(turn, d + slots - c, p))
+                nodes[REACH - d, p] = value * inside[-d]
+
+    def gather_above(turn):
         @pl.when(has_upper)
         def _():
             hop_copy(turn, 1, 1).wait_recv()
 
         for j in range(DEPTH2):
             for p in range(2):
-                at = REACH - 1 - DEPTH2 - j
-                nodes[at, p] = far_in[turn, 0, j, p] * inside[-1 - DEPTH2 - j]
-        for k in range(slots, slots + REACH):
-            for p in range(2):
-                near, far = upper_near(turn, k, p), upper_far(turn, k, p)
-                value = far if near is None else near if far is None else near + far
-                nodes[REACH + k, p] = value * inside[k]
+                at = slots + DEPTH2 + j
+                nodes[REACH + at, p] = far_in[turn, 1, j, p] * inside[at]
 
     wide = range(-DEPTH2, slots + DEPTH2)
 
@@ -370,8 +379,8 @@
             stack_high[(s,) + at] = high
             stack_low[(s,) + at] = low
 
-    def mix_nodes():
-        for k in wide:
+    def mix_nodes(places):
+        for k in places:
             plain, conjugate = mixes(nodes, REACH, k, 0)
             for p in range(2):
                 raised[k + DEPTH2, p] = plain[p]
@@ -391,21 +400,12 @@
             drive[at, 0] = (2 * second) * turned[at, 0] - beta * x_im
             drive[at, 1] = (2 * second) * turned[at, 1] + beta * x_re
 
+    half = slots // 2
     gather_near(0, x_ref)
-    gather_far(0)
-    mix_nodes()
-    turn_nodes(-DEPTH2, slots + 2 * DEPTH2)
-
-    @pl.when(edge)
-    def _():
-        for s in range(slots):
-            raw_copy(s).wait_recv()
-
-        @pl.when(has_lower)
-        def _():
-            hop_copy(1, 0, 1).start()
-
-        send_near(1, raw_in)
+    couple()
+    gather_below(0)
+    mix_nodes(range(-DEPTH2, half + DEPTH2))
+    turn_nodes(-DEPTH2, half + 2 * DEPTH2)
 
     def panel(q):
         return pl.ds(pl.multiple_of(q * rows, rows), rows)
@@ -423,9 +423,16 @@
 
     blocks = (ring - 2) * slots
 
+    early = (ring - 2) * half
+
+    def which(j):
+        group = j // early
+        rest = j - group * early
+        return rest // half, group * half + lax.rem(rest, half)
+
     def end_copy(way, j):
-        q = j // slots
-        return line_copy(way, ring - 1 - q if way == 0 else q, lax.rem(j, slots))
+        q, s = which(j)
+        return line_copy(way, ring - 1 - q if way == 0 else q, s)
 
     def feed_one(way, j):
         @pl.when((j >= WINDOW) & (j < blocks + WINDOW))
@@ -477,40 +484,61 @@
         real, imag = coeff[1, 0], coeff[1, 1]
         put_stack(s, 8, (real * x_re - imag * x_im, real * x_im + imag * x_re))
 
-    for s in range(slots):
+    def contribute(s):
         fill_stack(s)
         sums[s] = product(left_high[0], left_low[0], stack_high[s], stack_low[s])
-        feed(s)
-
-    for k in wide:
-        at = k + DEPTH2
-        x_re, x_im = nodes[k + REACH, 0], nodes[k + REACH, 1]
-        decay[at, 0] = (second * damping[k]) * x_im - second * turned[at, 0]
-        decay[at, 1] = -(second * damping[k]) * x_re - second * turned[at, 1]
-    for s in range(slots):
-        put_mixed(s, 0, (decay[s + DEPTH2, 0], decay[s + DEPTH2, 1]))
-        for mode in range(2):
-            _, conjugate = mixes(decay, DEPTH2, s, mode)
-            put_mixed(s, mode + 1, conjugate)
-    own[...] = right_product(0, slots)
-    for s in range(slots):
-        at = s + DEPTH2
-        rate = damping[s]
-        keep = 1.0 - step_size * rate + second * rate * rate
-        beta = step_size - second * rate
-        alive = inside[s] * number(s < count)
-        own_re = own[s, 0] + keep * nodes[s + REACH, 0] - beta * turned[at, 1]
-        own_im = own[s, 1] + keep * nodes[s + REACH, 1] + beta * turned[at, 0]
-        out_ref[s, 0] = alive * (own_re + sums[s, mine, :order]) + (1.0 - alive) * x_ref[s, 0]
-        out_ref[s, 1] = alive * (own_im + sums[s, mine, order:]) + (1.0 - alive) * x_ref[s, 1]
+
+    fed = min(WINDOW, early)
+    for s in range(half):
+        contribute(s)
+        for j in range(fed if s == half - 1 else s + 1):
+            if j >= s:
+                feed(j)
+    gather_above(0)
+    mix_nodes(range(half + DEPTH2, slots + DEPTH2))
+    turn_nodes(half + DEPTH2, half)
+    for s in range(half, slots):
+        contribute(s)
+
+    @pl.when(edge)
+    def _():
+        for s in range(slots):
+            raw_copy(s).wait_recv()
+
+        @pl.when(has_lower)
+        def _():
+            hop_copy(1, 0, 1).start()
+
+        send_near(1, raw_in)
+
+    def own_terms():
+        for k in wide:
+            at = k + DEPTH2
+            x_re, x_im = nodes[k + REACH, 0], nodes[k + REACH, 1]
+            decay[at, 0] = (second * damping[k]) * x_im - second * turned[at, 0]
+            decay[at, 1] = -(second * damping[k]) * x_re - second * turned[at, 1]
+        for s in range(slots):
+            put_mixed(s, 0, (decay[s + DEPTH2, 0], decay[s + DEPTH2, 1]))
+            for mode in range(2):
+                _, conjugate = mixes(decay, DEPTH2, s, mode)
+                put_mixed(s, mode + 1, conjugate)
+        own[...] = right_product(0, slots)
+        for s in range(slots):
+            at = s + DEPTH2
+            rate = damping[s]
+            keep = 1.0 - step_size * rate + second * rate * rate
+            beta = step_size - second * rate
+            own_re = own[s, 0] + keep * nodes[s + REACH, 0] - beta * turned[at, 1]
+            own_im = own[s, 1] + keep * nodes[s + REACH, 1] + beta * turned[at, 0]
+            total[s, 0] = own_re + sums[s, mine, :order]
+            total[s, 1] = own_im + sums[s, mine, order:]
 
     def pass_on(way, t):
         place = from_left if way == 0 else from_right
         passed = me if way == 0 else ring - 1 - me
         j = t - LAG * passed
         inner = (passed > 0) & (j >= 0) & (j < blocks)
-        s = lax.rem(jnp.maximum(j, 0), slots)
-        step = jnp.maximum(j, 0) // slots
+        step, s = which(jnp.maximum(j, 0))
         q = ring - 1 - step if way == 0 else step
 
         @pl.when(inner & (step < ring - 1 - passed))
@@ -523,14 +551,13 @@
         @pl.when(inner & (step == ring - 1 - passed))
         def _():
             line_copy(way, q, s).wait_recv()
-            alive = number((offset + s < live_total) & (s < count))
-            out_ref[s, 0] = out_ref[s, 0] + alive * place[q, s, :, :order]
-            out_ref[s, 1] = out_ref[s, 1] + alive * place[q, s, :, order:]
+            total[s, 0] = total[s, 0] + place[q, s, :, :order]
+            total[s, 1] = total[s, 1] + place[q, s, :, order:]
 
     def advance(t, carry):
         for way, passed in ((0, me), (1, ring - 1 - me)):
 
-            @pl.when((passed == 0) & (t >= slots))
+            @pl.when((passed == 0) & (t >= fed))
             def _():
                 feed_one(way, t)
 
@@ -541,28 +568,29 @@
     def act(s):
         fill_stack(s)
         value = product(left_high[1, mine, :], left_low[1, mine, :], stack_high[s], stack_low[s])
-        alive = inside[s] * number(s < count)
-        out_ref[s, 0] = out_ref[s, 0] + alive * value[:, :order]
-        out_ref[s, 1] = out_ref[s, 1] + alive * value[:, order:]
+        total[s, 0] = total[s, 0] + value[:, :order]
+        total[s, 1] = total[s, 1] + value[:, order:]
 
     def extra_near():
         gather_near(1, raw_in)
-        couple(raw_in)
+        couple()
 
     def extra_far():
-        gather_far(1)
-        mix_nodes()
-
-    half = slots // 2 + DEPTH2
+        gather_below(1)
+        gather_above(1)
+        mix_nodes(wide)
+
     extras = (
         (NEAR_AT, extra_near),
         (FAR_AT, extra_far),
-        (FAR_AT + 1, functools.partial(turn_nodes, -DEPTH2, half)),
-        (FAR_AT + 2, functools.partial(turn_nodes, half - DEPTH2, half)),
+        (FAR_AT + 1, functools.partial(turn_nodes, -DEPTH2, half + DEPTH2)),
+        (FAR_AT + 2, functools.partial(turn_nodes, half, half + DEPTH2)),
         (FAR_AT + 3, lambda: [act(s) for s in range(slots // 2)]),
         (FAR_AT + 4, lambda: [act(s) for s in range(slots // 2, slots)]),
     )
-    begin = 0
+    lax.fori_loop(0, OWN_AT, advance, 0)
+    own_terms()
+    begin = OWN_AT
     for at, extra in extras:
         lax.fori_loop(begin, at, advance, 0)
         begin = at
@@ -572,6 +600,11 @@
             extra()
 
     lax.fori_loop(begin, blocks + max(WINDOW, LAG * (ring - 1)), advance, 0)
+    for s in range(slots):
+        alive = number((offset + s < live_total) & (s < count))
+        for p in range(2):
+            value = chosen(lambda c: total[s + slots - c, p] if s < c else None)
+            out_ref[s, p] = alive * value + (1.0 - alive) * x_ref[s, p]
 
     @pl.when(jnp.logical_not(has_left & has_right))
     def _():
@@ -642,6 +675,7 @@
                 pltpu.VMEM((slots, 9 * rows, 2 * order), bf16),
                 pltpu.VMEM((slots, order, 2 * order), f32),
                 pltpu.VMEM((slots, *block), f32),
+                pltpu.VMEM((slots, *block), f32),
                 pltpu.VMEM((ring, slots, rows, 2 * order), f32),
                 pltpu.VMEM((ring, slots, rows, 2 * order), f32),
                 dma((slots,)),

time: 53.2 us -> 51.7 us (0.972); the launches traced: 53 us -> 50.7 us
  Pallas kernels: 51.1 us -> 48.8 us
    pallas_call x1, Pallas kernels: 51.1 us -> 48.8 us  [on_device(): pl.pallas_call(functools.partial(kernel, shards, ring), out_shape=jax.Sha...]
where the time goes in v4:
time: 51.7 us; the launch traced here: 50.7 us
  Pallas kernels  48.8 us (94%)
  local copies, waits for them, and re-layouts  1.87 us (4%)
    pallas_call x1, Pallas kernels, on_device(): pl.pallas_call(functools.partial(kernel, shards, ring), out_shape=jax.Sha...  48.8 us
    unnamed x1, local copies, waits for them, and re-layouts  1.87 us

profile of v4, /device:TPU:12, one launch (start us, length us, event | category | flops | bytes accessed | tf_op | source)
XLA Modules:
  0.0 50.7 jit_solution(1308309451824626733)
XLA Ops:
  0.0 48.8 %shard_map.64 = f32[4,2,64,256]{3,2,1,0:T(8,128)} custom-call(s32[8]{0:T(128)} %counts.1, f32[2]{0:T(128)} %gamma.1, f32[2,2]{1,0:T(2,128)} %coeff.1, f32[4,2,64,256]{3,2,1,0:T(8,128)} %x_hbm.1, f32[256,256]{1,0:T(8,128)} %h_hbm.1, f32[2,256,256]{2,1,0:T(8,128)} %q_hbm.1), custom_call_target="tpu_custom_call" | custom-call | tf_op jit(solution)/shard_map/pallas_call | solution.py:648
  48.8 1.9 %copy.8 = f32[4,2,64,256]{3,2,1,0:T(8,128)} copy(f32[4,2,64,256]{3,2,1,0:T(8,128)} %shard_map.64) | data formatting | bytes 1048576

commit v5 on v4

--- a/solution.py
+++ b/solution.py
@@ -11,9 +11,9 @@
 REACH = 2 * DEPTH2
 WINDOW = 4
 LAG = 2
-OWN_AT = 3
-NEAR_AT = 5
-FAR_AT = 8
+LATE_AT = 3
+NEAR_AT = 6
+FAR_AT = 9
 MESH = pl.DeviceIdType.MESH
 step_size = 0.2
 second = step_size * 0.5 * step_size
@@ -403,9 +403,11 @@
     half = slots // 2
     gather_near(0, x_ref)
     couple()
+    mix_nodes(range(half, slots))
+    turn_nodes(half, slots - half)
     gather_below(0)
-    mix_nodes(range(-DEPTH2, half + DEPTH2))
-    turn_nodes(-DEPTH2, half + 2 * DEPTH2)
+    mix_nodes(range(-DEPTH2, half))
+    turn_nodes(-DEPTH2, half + DEPTH2)
 
     def panel(q):
         return pl.ds(pl.multiple_of(q * rows, rows), rows)
@@ -494,11 +496,15 @@
         for j in range(fed if s == half - 1 else s + 1):
             if j >= s:
                 feed(j)
-    gather_above(0)
-    mix_nodes(range(half + DEPTH2, slots + DEPTH2))
-    turn_nodes(half + DEPTH2, half)
-    for s in range(half, slots):
-        contribute(s)
+    def late_turn():
+        gather_above(0)
+        mix_nodes(range(slots, slots + DEPTH2))
+        turn_nodes(slots, DEPTH2)
+        contribute(half)
+
+    def late_rest():
+        for s in range(half + 1, slots):
+            contribute(s)
 
     @pl.when(edge)
     def _():
@@ -588,9 +594,11 @@
         (FAR_AT + 3, lambda: [act(s) for s in range(slots // 2)]),
         (FAR_AT + 4, lambda: [act(s) for s in range(slots // 2, slots)]),
     )
-    lax.fori_loop(0, OWN_AT, advance, 0)
-    own_terms()
-    begin = OWN_AT
+    begin = 0
+    for at, stage in ((LATE_AT, late_turn), (LATE_AT + 1, late_rest), (LATE_AT + 2, own_terms)):
+        lax.fori_loop(begin, at, advance, 0)
+        begin = at
+        stage()
     for at, extra in extras:
         lax.fori_loop(begin, at, advance, 0)
         begin = at

time: 51.7 us -> 51.1 us (0.988); the launches traced: 50.7 us -> 50.9 us
  no operation moved by 1% of the time
where the time goes in v5:
time: 51.1 us; the launch traced here: 50.9 us
  Pallas kernels  49 us (96%)
  local copies, waits for them, and re-layouts  1.87 us (4%)
    pallas_call x1, Pallas kernels, on_device(): pl.pallas_call(functools.partial(kernel, shards, ring), out_shape=jax.Sha...  49 us
    unnamed x1, local copies, waits for them, and re-layouts  1.87 us

profile of v5, /device:TPU:12, one launch (start us, length us, event | category | flops | bytes accessed | tf_op | source)
XLA Modules:
  0.0 50.9 jit_solution(13468768965976495037)
XLA Ops:
  0.0 49.0 %shard_map.64 = f32[4,2,64,256]{3,2,1,0:T(8,128)} custom-call(s32[8]{0:T(128)} %counts.1, f32[2]{0:T(128)} %gamma.1, f32[2,2]{1,0:T(2,128)} %coeff.1, f32[4,2,64,256]{3,2,1,0:T(8,128)} %x_hbm.1, f32[256,256]{1,0:T(8,128)} %h_hbm.1, f32[2,256,256]{2,1,0:T(8,128)} %q_hbm.1), custom_call_target="tpu_custom_call" | custom-call | tf_op jit(solution)/shard_map/pallas_call | solution.py:656
  49.0 1.9 %copy.8 = f32[4,2,64,256]{3,2,1,0:T(8,128)} copy(f32[4,2,64,256]{3,2,1,0:T(8,128)} %shard_map.64) | data formatting | bytes 1048576
